TPU v7x, 32 devices: a whole 2x2x4 slice. The times are simulated.
32 devices in a mesh: groups: 2 (over y), space: 8 (over z, x), section: 2 (over core).
Axes of the slice: x: 2, y: 2, z: 4, core: 2. Of those that a mesh axis runs over, the one named last changes fastest.
Arguments:
- atm_state: bfloat16 [4, 8, 256, 256], P(('groups', 'section'), 'space'), parts along dimension 0, may hold values from -6 to 6
- ocean_state: bfloat16 [4, 2048, 192], P(('groups', 'section'), 'space'), parts along dimension 0, may hold values from -6 to 6
- owners: int32 [8, 256, 2], P('space'), may hold values from 0 to 7, all different within a row; in each aligned block of 256 rows (0 to 255, 256 to 511, ..., all dimensions but the last counted through in order) at most 128 rows name the same one
- target_cell: int32 [8, 256, 2], P('space'), may hold values from 0 to 255
- margin_weight: float32 [8, 256, 2], P('space'), may hold values from 0.25 to 1
- sea_mask: int32 [8, 256], P('space'), may hold values 0 or 1
- conv_kernel: bfloat16 [9, 256, 256], replicated, may hold values from -0.125 to 0.125
- meridional_weight: bfloat16 [256, 256], replicated, may hold values from -0.375 to 0.375
- atm_gain: float32 [256], replicated, may hold values from 0.25 to 1.75
- atm_in: bfloat16 [256, 1024], replicated, may hold values from -0.375 to 0.375
- atm_out: bfloat16 [1024, 256], replicated, may hold values from -0.1875 to 0.1875
- flux_weight: bfloat16 [256, 128], replicated, may hold values from -0.375 to 0.375
- forcing_weight: bfloat16 [128, 192], replicated, may hold values from -0.5 to 0.5
- ocean_gain: float32 [192], replicated, may hold values from 0.25 to 1.75
- ocean_in: bfloat16 [192, 768], replicated, may hold values from -0.4375 to 0.4375
- ocean_out: bfloat16 [768, 192], replicated, may hold values from -0.21875 to 0.21875
- surface_weight: bfloat16 [192, 128], replicated, may hold values from -0.4375 to 0.4375
- feedback_weight: bfloat16 [128, 256], replicated, may hold values from -0.5 to 0.5
Outputs:
- atm_next: bfloat16 [4, 8, 256, 256], P(('groups', 'section'), 'space'), parts along dimension 0
- ocean_next: bfloat16 [4, 2048, 192], P(('groups', 'section'), 'space'), parts along dimension 0
There are 2 independent parts, one for each index of `groups`. A program takes and returns all parts, laid end to end along the dimension named above; an argument that names none is the same for every part. Nothing has to cross between parts.
Inputs may be any that keep to these rules, and one draw needn't show every extreme that they name: Within the 256 cells of one latitude band, no owner is named by more than 128 margin entries, a bound that some block reaches; the 2 owners of one cell differ.
All inputs are finite; a program needn't handle non-finite values. No bound on the sum of `sea_mask` on one device may be relied on, other than what follows from the above.
Results may differ from a plain program's by a relative error of at most 0.014.
Values may be sent and summed in bfloat16 or wider, within the bound.
A program may use at most 64 MiB of HBM per device.

v0:
```python
import math
import jax
import jax.numpy as jnp
from jax import lax
from jax.sharding import PartitionSpec as P


def extended(cells, sides, width):
    for axis, dim in sides:
        count = lax.axis_size(axis)
        ends = count - 1
        head = lax.slice_in_dim(cells, 0, width, axis=dim)
        tail = lax.slice_in_dim(cells, cells.shape[dim] - width, cells.shape[dim], axis=dim)
        cells = jnp.concatenate(
            [
                lax.ppermute(tail, axis, [(i, (i + 1) % count) for i in range(ends)]),
                cells,
                lax.ppermute(head, axis, [((i + 1) % count, i) for i in range(ends)]),
            ],
            axis=dim,
        )
    return cells


def entering(part, axis, combine, identity):
    place = lax.axis_index(axis)
    gathered = lax.all_gather(part, axis)
    state = jnp.zeros_like(part) + jnp.asarray(identity, part.dtype)

    def one(hop, state):
        return combine(state, lax.dynamic_index_in_dim(gathered, hop, 0, False))

    return lax.fori_loop(0, place, one, state)


def conv_taps(padded, kernel, lat_rows):
    channels = padded.shape[-1]
    columns = []
    for row_off in range(3):
        lat_band = padded[row_off : row_off + lat_rows]
        for col_off in range(3):
            columns.append(jnp.roll(lat_band, 1 - col_off, axis=1))
    stacked = jnp.concatenate(columns, axis=-1)
    flattened = stacked.reshape(-1, 9 * channels)
    result = jnp.dot(
        flattened, kernel.reshape(9 * channels, channels), preferred_element_type=jnp.float32
    )
    return result.reshape(lat_rows, padded.shape[1], channels)


def rms_scale(values, gain_vec):
    return values * lax.rsqrt(jnp.mean(values * values, axis=-1, keepdims=True) + 1e-06) * gain_vec


def add_terms(earlier, later):
    return earlier + later


def contract_first(left, right):
    return lax.dot_general(
        left, right, (((0,), (0,)), ((), ())), preferred_element_type=jnp.float32
    )


def local(
    atm_state,
    ocean_state,
    owners,
    target_cell,
    margin_weight,
    sea_mask,
    conv_kernel,
    meridional_weight,
    atm_gain,
    atm_in,
    atm_out,
    flux_weight,
    forcing_weight,
    ocean_gain,
    ocean_in,
    ocean_out,
    surface_weight,
    feedback_weight,
):
    atm_one = atm_state[0]
    ocn_one = ocean_state[0]
    lat_rows, lon_cells, channels = atm_one.shape
    margin_count = owners.shape[-1]
    flux_width = flux_weight.shape[1]
    peer_count = lax.axis_size("space")
    slot_count = max(2, 2 * lat_rows * lon_cells * margin_count // peer_count)
    lat_total = lat_rows * peer_count
    padded = extended(atm_one, (("space", 0),), 1)
    mixing = conv_taps(padded, conv_kernel, lat_rows)
    hidden = atm_one.astype(jnp.float32) + mixing
    zonal_sums = jnp.sum(hidden, axis=1) / math.sqrt(lon_cells)
    band_total = jnp.sum(zonal_sums, axis=0)
    before = entering(band_total, "space", add_terms, jnp.zeros_like(band_total))
    prefix = (before[None, :] + jnp.cumsum(zonal_sums, axis=0) - zonal_sums) / math.sqrt(lat_total)
    meridional = jnp.dot(
        prefix, meridional_weight.astype(jnp.float32), precision=lax.Precision.HIGHEST
    )
    lifted = (hidden + meridional[:, None, :]).reshape(-1, channels)
    normed = rms_scale(lifted, atm_gain).astype(jnp.bfloat16)
    activated = jax.nn.silu(jnp.dot(normed, atm_in, preferred_element_type=jnp.float32)).astype(
        jnp.bfloat16
    )
    atm_mid = (lifted + jnp.dot(activated, atm_out, preferred_element_type=jnp.float32)).astype(
        jnp.bfloat16
    )
    flux_rows = jnp.dot(atm_mid, flux_weight, preferred_element_type=jnp.float32)
    sea_cells = sea_mask.astype(jnp.float32).reshape(-1)
    weights = margin_weight.reshape(-1, margin_count)
    payload = (weights[:, :, None] * sea_cells[:, None, None] * flux_rows[:, None, :]).astype(
        jnp.bfloat16
    )
    payload = payload.reshape(-1, flux_width)
    owner_ids = owners.reshape(-1)
    owner_hits = (owner_ids[:, None] == jnp.arange(peer_count, dtype=jnp.int32)[None, :]).astype(
        jnp.int32
    )
    slot_rank = jnp.sum((jnp.cumsum(owner_hits, axis=0) - 1) * owner_hits, axis=1)
    slot_index = owner_ids * slot_count + slot_rank
    slot_total = peer_count * slot_count
    placement = slot_index[:, None] == jnp.arange(slot_total, dtype=jnp.int32)[None, :]
    place_bf = placement.astype(jnp.bfloat16)
    send_rows = contract_first(place_bf, payload).astype(jnp.bfloat16)
    entry_cells = target_cell.reshape(-1)
    send_cells = jnp.sum(placement.astype(jnp.int32) * entry_cells[:, None], axis=0)
    recv_rows, recv_cells = (
        lax.all_to_all(
            send_rows.reshape(peer_count, slot_count, flux_width),
            "space",
            split_axis=0,
            concat_axis=0,
            tiled=True,
        ),
        lax.all_to_all(
            send_cells.reshape(peer_count, slot_count),
            "space",
            split_axis=0,
            concat_axis=0,
            tiled=True,
        ),
    )
    recv_cells = recv_cells.reshape(-1)
    ocean_cells = ocn_one.shape[0]
    cell_onehot = (recv_cells[:, None] == jnp.arange(ocean_cells, dtype=jnp.int32)[None, :]).astype(
        jnp.bfloat16
    )
    forcing = contract_first(cell_onehot, recv_rows.reshape(-1, flux_width)).astype(jnp.bfloat16)
    ocean_lift = ocn_one.astype(jnp.float32) + jnp.dot(
        forcing, forcing_weight, preferred_element_type=jnp.float32
    )
    ocean_normed = rms_scale(ocean_lift, ocean_gain).astype(jnp.bfloat16)
    ocean_act = jax.nn.silu(
        jnp.dot(ocean_normed, ocean_in, preferred_element_type=jnp.float32)
    ).astype(jnp.bfloat16)
    ocean_new = (
        ocean_lift + jnp.dot(ocean_act, ocean_out, preferred_element_type=jnp.float32)
    ).astype(jnp.bfloat16)
    surface = jnp.dot(ocean_new, surface_weight, preferred_element_type=jnp.float32).astype(
        jnp.bfloat16
    )
    back_rows = jnp.dot(cell_onehot, surface, preferred_element_type=jnp.float32).astype(
        jnp.bfloat16
    )
    returned = lax.all_to_all(
        back_rows.reshape(peer_count, slot_count, flux_width),
        "space",
        split_axis=0,
        concat_axis=0,
        tiled=True,
    )
    picked = jnp.dot(place_bf, returned.reshape(-1, flux_width), preferred_element_type=jnp.float32)
    picked = picked.reshape(-1, margin_count, flux_width)
    feedback = jnp.sum(weights[:, :, None] * picked, axis=1).astype(jnp.bfloat16)
    back_term = jnp.dot(feedback, feedback_weight, preferred_element_type=jnp.float32)
    atm_new = (atm_mid.astype(jnp.float32) + sea_cells[:, None] * back_term).astype(jnp.bfloat16)
    return (atm_new.reshape(1, lat_rows, lon_cells, channels), ocean_new[None])


def solution(mesh):
    placed = (
        P(("groups", "section"), "space", None, None),
        P(("groups", "section"), "space", None),
        P("space", None, None),
        P("space", None, None),
        P("space", None, None),
        P("space", None),
        P(),
        P(),
        P(),
        P(),
        P(),
        P(),
        P(),
        P(),
        P(),
        P(),
        P(),
        P(),
    )
    return jax.shard_map(
        local,
        mesh=mesh,
        in_specs=placed,
        out_specs=(
            P(("groups", "section"), "space", None, None),
            P(("groups", "section"), "space", None),
        ),
        check_vma=False,
    )
```

profile of v0, /device:TPU:0, one launch (start us, length us, event | category | flops | bytes accessed | tf_op | source)
XLA Modules:
  0.0 71.0 jit_solution(671286517310417763)
XLA Ops:
  0.7 5.0 %collective-permute-start = (bf16[1,256,256]{2,1,0:T(8,128)(2,1)}, bf16[1,256,256]{2,1,0:T(8,128)(2,1)S(1)}, u32[]{:S(2)}, u32[]{:S(2)}) collective-permute-start(bf16[1,256,256]{2,1,0:T(8,128)(2,1)} %bitcast.71), channel_id=1, source_target_pairs={{0,2},{2,4},{4,6},{6,8},{8,10},{10,12},{12,14},{1,3},{3,5},{5,7},{... | collective-permute-start | bytes 393224 | tf_op jit(solution)/shard_map/ppermute | solution.py:16
  5.7 1.3 %collective-permute-start.1 = (bf16[1,256,256]{2,1,0:T(8,128)(2,1)}, bf16[1,256,256]{2,1,0:T(8,128)(2,1)S(1)}, u32[]{:S(2)}, u32[]{:S(2)}) collective-permute-start(bf16[1,256,256]{2,1,0:T(8,128)(2,1)} %bitcast.72), channel_id=1, source_target_pairs={{2,0},{4,2},{6,4},{8,6},{10,8},{12,10},{14,12},{3,1},{5,3},{7,5},{... | collective-permute-start | bytes 393224 | tf_op jit(solution)/shard_map/ppermute | solution.py:18
  7.0 0.8 %copy.35 = s32[1,256,2]{2,1,0:T(8,128)S(1)} copy(s32[1,256,2]{1,2,0:T(2,128)} %param.22) | data formatting | bytes 4096 | tf_op args[2]
  8.1 1.1 %reduce-window.6 = s32[8,4,128]{2,0,1:T(8,128)S(1)} reduce-window(s32[8,4,128]{2,0,1:T(8,128)S(1)} %fusion.41, s32[]{:T(128)} %constant.39.clone.1), window={size=1x1x128 pad=0_0x0_0x127_0}, to_apply=%region_4.5 | reduce-window | flops 520192 | bytes 32772 | tf_op jit(solution)/shard_map/reduce-window
  9.3 0.2 slice_reduce_fusion
  9.6 0.8 %copy.39 = s32[1,256,2]{2,1,0:T(8,128)S(1)} copy(s32[1,256,2]{1,2,0:T(2,128)} %param.23) | data formatting | bytes 4096 | tf_op args[3]
  10.6 0.9 %select_reduce_fusion = s32[1024]{0:T(1024)} fusion(s32[512]{0:T(512)S(1)} %mul.144, s32[512]{0:T(512)S(1)} %multiply_add_fusion), kind=kLoop, calls=%fused_computation.1 | loop fusion | flops 1571840 | bytes 8192 | tf_op jit(solution)/shard_map/reduce_sum | solution.py:129
  11.5 7.0 %all-to-all-start = ((s32[8,1,128]{2,1,0:T(1,128)}), s32[8,1,128]{2,1,0:T(1,128)S(1)}, u32[]{:S(2)}, u32[]{:S(2)}) async-start(s32[8,1,128]{2,1,0:T(1,128)} %bitcast.14), calls=%async_computation | async-start | bytes 8192 | tf_op jit(solution)/shard_map/all_to_all | solution.py:138
  18.4 1.0 %fusion.47 = (bf16[1,255,256]{2,1,0:T(8,128)(2,1)S(1)}, bf16[1,255,256]{2,1,0:T(8,128)(2,1)S(1)}) fusion(bf16[1,256,256]{2,1,0:T(8,128)(2,1)} %bitcast.73), kind=kLoop, calls=%fused_computation.73 | loop fusion | bytes 522240 | tf_op jit(solution)/shard_map/jit(_roll_static)/slice | solution.py:42
  20.5 0.5 fusion.51
  21.0 21.0 %all-gather.1 = f32[8,1,256]{2,1,0:T(1,128)S(1)} all-gather(f32[1,1,256]{2,1,0:T(1,128)S(1)} %bitcast.86), channel_id=2, replica_groups=mesh['groups'=2,'space'=8,'section'=2] {'space'}, dimensions={0}, use_global_device_ids=true | all-gather | bytes 9216 | tf_op jit(solution)/shard_map/all_gather | solution.py:27
  42.2 0.2 multiply_reduce_fusion
  42.4 0.6 fusion.18
  43.0 0.2 copy-done.3
  43.2 0.2 fusion.53
  43.5 0.9 %fusion.4 = bf16[1024,128]{1,0:T(8,128)(2,1)S(1)} fusion(s32[512]{0:T(512)S(1)} %multiply_add_fusion, f32[512,128]{1,0:T(8,128)S(1)} %bitcast.75, f32[512]{0:T(512)S(1)} %mul.149), kind=kOutput, calls=%fused_computation.7 | convolution fusion | flops 135004160 | bytes 528384 | tf_op jit(solution)/shard_map/dot_general | solution.py:60
  44.4 10.6 %all_to_all.19 = bf16[8,128,128]{2,1,0:T(8,128)(2,1)S(1)} all-to-all(bf16[8,128,128]{2,1,0:T(8,128)(2,1)S(1)} %bitcast.77), channel_id=1, replica_groups=mesh['groups'=2,'space'=8,'section'=2] {'space'}, dimensions={0} | all-to-all | bytes 524288 | tf_op jit(solution)/shard_map/all_to_all | solution.py:131
  55.1 0.8 %multiply_reduce_fusion.1 = (f32[256]{0:T(256)S(1)}, f32[256,192]{0,1:T(8,128)S(1)}) fusion(bf16[128,192]{0,1:T(8,128)(2,1)S(1)} %copy-done.12, bf16[1024,128]{1,0:T(8,128)(2,1)S(1)} %bitcast.78, s32[1024]{0:T(1024)S(1)} %bitcast.87, bf16[1,256,192]{1,2,0:T(8,128)(2,1)S(1)} %copy-done.11), kind=kOutput, calls=%fused_computation.37 | convolution fusion | flops 80183040 | bytes 611328 | tf_op jit(solution)/shard_map/dot_general | solution.py:152
  55.9 0.7 fusion.19
  56.7 1.2 %convolution_convert_fusion = bf16[1024,128]{1,0:T(8,128)(2,1)} fusion(bf16[256,192]{0,1:T(8,128)(2,1)S(1)} %fusion.19, bf16[192,128]{1,0:T(8,128)(2,1)S(1)} %copy-done.13, s32[1024]{0:T(1024)S(1)} %bitcast.88), kind=kOutput, calls=%fused_computation.8 | convolution fusion | flops 80117760 | bytes 413696 | tf_op jit(solution)/shard_map/dot_general | solution.py:165
  58.0 3.5 %all-to-all-start.2 = ((bf16[8,128,128]{2,1,0:T(8,128)(2,1)}), bf16[8,128,128]{2,1,0:T(8,128)(2,1)S(1)}, u32[]{:S(2)}, u32[]{:S(2)}) async-start(bf16[8,128,128]{2,1,0:T(8,128)(2,1)} %bitcast.20), calls=%async_computation.2 | async-start | bytes 524288 | tf_op jit(solution)/shard_map/all_to_all | solution.py:168
  61.8 7.9 %all-to-all-done.2 = bf16[8,128,128]{2,1,0:T(8,128)(2,1)S(1)} async-done(((bf16[8,128,128]{2,1,0:T(8,128)(2,1)}), bf16[8,128,128]{2,1,0:T(8,128)(2,1)S(1)}, u32[]{:S(2)}, u32[]{:S(2)}) %all-to-all-start.2) | async-done | bytes 262176 | tf_op jit(solution)/shard_map/all_to_all | solution.py:168
  69.7 0.5 fusion.15
  70.2 0.8 %fusion.20 = bf16[1,1,256,256]{3,2,1,0:T(8,128)(2,1)} fusion(bf16[128,256]{1,0:T(8,128)(2,1)S(1)} %copy-done.4, bf16[256,256]{1,0:T(8,128)(2,1)S(1)} %fusion.18, f32[256]{0:T(256)S(1)} %bitcast.82, bf16[256,128]{1,0:T(8,128)(2,1)S(1)} %fusion.15), kind=kOutput, calls=%fused_computation.22 | convolution fusion | flops 17039360 | bytes 394240 | tf_op jit(solution)/shard_map/dot_general | solution.py:178
  (76 shorter events, 2.0 us)
Async XLA Ops:
  0.6 19.8 %copy-start = (bf16[9,256,256]{2,1,0:T(8,128)(2,1)S(1)}, bf16[9,256,256]{2,1,0:T(8,128)(2,1)}, u32[]{:S(2)}) copy-start(bf16[9,256,256]{2,1,0:T(8,128)(2,1)} %param.26) | copy-start | bytes 3538948
  0.6 19.4 %copy-start.1 = (bf16[1,1,256,256]{3,2,1,0:T(8,128)(2,1)S(1)}, bf16[1,1,256,256]{3,2,1,0:T(8,128)(2,1)}, u32[]{:S(2)}) copy-start(bf16[1,1,256,256]{3,2,1,0:T(8,128)(2,1)} %param.20) | copy-start | bytes 393220
  0.7 18.8 %copy-start.6 = (s32[1,256]{1,0:T(1,128)S(1)}, s32[1,256]{1,0:T(1,128)}, u32[]{:S(2)}) copy-start(s32[1,256]{1,0:T(1,128)} %param.25) | copy-start | bytes 3076
  0.7 19.1 %copy-start.5 = (f32[1,256,2]{1,2,0:T(2,128)S(1)}, f32[1,256,2]{1,2,0:T(2,128)}, u32[]{:S(2)}) copy-start(f32[1,256,2]{1,2,0:T(2,128)} %param.24) | copy-start | bytes 6148
  0.7 19.4 %collective-permute-start = (bf16[1,256,256]{2,1,0:T(8,128)(2,1)}, bf16[1,256,256]{2,1,0:T(8,128)(2,1)S(1)}, u32[]{:S(2)}, u32[]{:S(2)}) collective-permute-start(bf16[1,256,256]{2,1,0:T(8,128)(2,1)} %bitcast.71), channel_id=1, source_target_pairs={{0,2},{2,4},{4,6},{6,8},{8,10},{10,12},{12,14},{1,3},{3,5},{5,7},{... | collective-permute-start | bytes 393224 | tf_op jit(solution)/shard_map/ppermute | solution.py:16
  5.7 14.6 %collective-permute-start.1 = (bf16[1,256,256]{2,1,0:T(8,128)(2,1)}, bf16[1,256,256]{2,1,0:T(8,128)(2,1)S(1)}, u32[]{:S(2)}, u32[]{:S(2)}) collective-permute-start(bf16[1,256,256]{2,1,0:T(8,128)(2,1)} %bitcast.72), channel_id=1, source_target_pairs={{2,0},{4,2},{6,4},{8,6},{10,8},{12,10},{14,12},{3,1},{5,3},{7,5},{... | collective-permute-start | bytes 393224 | tf_op jit(solution)/shard_map/ppermute | solution.py:18
  11.5 32.9 %all-to-all-start = ((s32[8,1,128]{2,1,0:T(1,128)}), s32[8,1,128]{2,1,0:T(1,128)S(1)}, u32[]{:S(2)}, u32[]{:S(2)}) async-start(s32[8,1,128]{2,1,0:T(1,128)} %bitcast.14), calls=%async_computation | async-start | bytes 8192 | tf_op jit(solution)/shard_map/all_to_all | solution.py:138
  20.4 21.6 %copy-start.2 = (bf16[256,256]{1,0:T(8,128)(2,1)S(1)}, bf16[256,256]{1,0:T(8,128)(2,1)}, u32[]{:S(2)}) copy-start(bf16[256,256]{1,0:T(8,128)(2,1)} %param.27) | copy-start | bytes 393220
  20.5 21.9 %copy-start.7 = (bf16[1024,256]{1,0:T(8,128)(2,1)S(1)}, bf16[1024,256]{1,0:T(8,128)(2,1)}, u32[]{:S(2)}) copy-start(bf16[1024,256]{1,0:T(8,128)(2,1)} %param.30) | copy-start | bytes 1572868
  20.5 21.9 %copy-start.8 = (bf16[256,1024]{1,0:T(8,128)(2,1)S(1)}, bf16[256,1024]{1,0:T(8,128)(2,1)}, u32[]{:S(2)}) copy-start(bf16[256,1024]{1,0:T(8,128)(2,1)} %param.29) | copy-start | bytes 1572868
  20.5 21.9 %copy-start.14 = (f32[256]{0:T(256)S(1)}, f32[256]{0:T(256)}, u32[]{:S(2)}) copy-start(f32[256]{0:T(256)} %param.28) | copy-start | bytes 3076
  42.4 0.8 %copy-start.3 = (bf16[256,128]{1,0:T(8,128)(2,1)S(1)}, bf16[256,128]{1,0:T(8,128)(2,1)}, u32[]{:S(2)}) copy-start(bf16[256,128]{1,0:T(8,128)(2,1)} %param.31) | copy-start | bytes 196612
  43.2 11.9 %copy-start.11 = (bf16[1,256,192]{1,2,0:T(8,128)(2,1)S(1)}, bf16[1,256,192]{1,2,0:T(8,128)(2,1)}, u32[]{:S(2)}) copy-start(bf16[1,256,192]{1,2,0:T(8,128)(2,1)} %param.21) | copy-start | bytes 294916
  43.2 11.9 %copy-start.12 = (bf16[128,192]{0,1:T(8,128)(2,1)S(1)}, bf16[128,192]{0,1:T(8,128)(2,1)}, u32[]{:S(2)}) copy-start(bf16[128,192]{0,1:T(8,128)(2,1)} %param.32) | copy-start | bytes 147460
  43.5 12.4 %copy-start.9 = (bf16[768,192]{0,1:T(8,128)(2,1)S(1)}, bf16[768,192]{0,1:T(8,128)(2,1)}, u32[]{:S(2)}) copy-start(bf16[768,192]{0,1:T(8,128)(2,1)} %param.35) | copy-start | bytes 884740
  43.5 12.4 %copy-start.10 = (bf16[192,768]{1,0:T(8,128)(2,1)S(1)}, bf16[192,768]{1,0:T(8,128)(2,1)}, u32[]{:S(2)}) copy-start(bf16[192,768]{1,0:T(8,128)(2,1)} %param.34) | copy-start | bytes 884740
  43.5 12.4 %copy-start.15 = (f32[192]{0:T(256)S(1)}, f32[192]{0:T(256)}, u32[]{:S(2)}) copy-start(f32[192]{0:T(256)} %param.33) | copy-start | bytes 2308
  55.9 0.8 %copy-start.13 = (bf16[192,128]{1,0:T(8,128)(2,1)S(1)}, bf16[192,128]{1,0:T(8,128)(2,1)}, u32[]{:S(2)}) copy-start(bf16[192,128]{1,0:T(8,128)(2,1)} %param.36) | copy-start | bytes 147460
  56.7 13.5 %copy-start.16 = (bf16[256,192]{0,1:T(8,128)(2,1)}, bf16[256,192]{0,1:T(8,128)(2,1)S(1)}, u32[]{:S(2)}) copy-start(bf16[256,192]{0,1:T(8,128)(2,1)S(1)} %fusion.19) | copy-start | bytes 294916
  58.0 12.2 %copy-start.4 = (bf16[128,256]{1,0:T(8,128)(2,1)S(1)}, bf16[128,256]{1,0:T(8,128)(2,1)}, u32[]{:S(2)}) copy-start(bf16[128,256]{1,0:T(8,128)(2,1)} %param.37) | copy-start | bytes 196612
  58.0 11.7 %all-to-all-start.2 = ((bf16[8,128,128]{2,1,0:T(8,128)(2,1)}), bf16[8,128,128]{2,1,0:T(8,128)(2,1)S(1)}, u32[]{:S(2)}, u32[]{:S(2)}) async-start(bf16[8,128,128]{2,1,0:T(8,128)(2,1)} %bitcast.20), calls=%async_computation.2 | async-start | bytes 524288 | tf_op jit(solution)/shard_map/all_to_all | solution.py:168
where the time goes:
time: 71.6 us; the launch traced here: 71 us
  blocking collectives  31.6 us (44%)
  starting transfers between devices  16.8 us (23%)
  waiting for transfers between devices  7.92 us (11%)
  matrix products  6.33 us (9%)
  local copies, waits for them, and re-layouts  4.64 us (6%)
  other arithmetic  2.53 us (4%)
  between operations  1.17 us (2%)
    all_gather x1, blocking collectives, entering(): gathered = lax.all_gather(part, axis)  21 us
    all_to_all x1, blocking collectives, local(): lax.all_to_all(send_rows.reshape(peer_count, slot_count, flux_width), 'sp...  10.6 us
    all_to_all x1, waiting for transfers between devices, local(): lax.all_to_all(back_rows.reshape(peer_count, slot_count, flux_width), 'sp...  7.91 us
    all_to_all x1, starting transfers between devices, local(): lax.all_to_all(send_cells.reshape(peer_count, slot_count), 'space', split...  6.96 us
    ppermute x1, starting transfers between devices, extended(): lax.ppermute(tail, axis, [(i, (i + 1) % count) for i in range(ends)])  5.01 us
    all_to_all x1, starting transfers between devices, local(): lax.all_to_all(back_rows.reshape(peer_count, slot_count, flux_width), 'sp...  3.54 us
    unnamed x41, local copies, waits for them, and re-layouts  2.22 us
  transfers between devices with their start and end apart: 4, of which 1 were waited for; matrix products, arithmetic and copies ran while one was open for 13% of the time, Pallas kernels for 0%

commit v1 on v0

--- a/solution.py
+++ b/solution.py
@@ -3,6 +3,29 @@
 import jax.numpy as jnp
 from jax import lax
 from jax.sharding import PartitionSpec as P
+
+
+def cut_along(value, dim, peers):
+    shape = value.shape
+    blocks = value.reshape(*shape[:dim], peers, shape[dim] // peers, *shape[dim + 1 :])
+    return jnp.moveaxis(blocks, dim, 0)
+
+
+def joined_along(blocks, dim):
+    blocks = jnp.moveaxis(blocks, 0, dim)
+    shape = blocks.shape
+    return blocks.reshape(*shape[:dim], shape[dim] * shape[dim + 1], *shape[dim + 2 :])
+
+
+def sent_to_each(x, axis, split_dim, concat_dim):
+    count, mine = (lax.axis_size(axis), lax.axis_index(axis))
+    tiles = cut_along(x, split_dim, count)
+    done = [tiles[mine]]
+    for step in range(1, count):
+        sent = tiles[(mine + step) % count]
+        done.append(lax.ppermute(sent, axis, [(i, (i + step) % count) for i in range(count)]))
+    tiles = jnp.stack(done)[(mine - jnp.arange(count)) % count]
+    return joined_along(tiles, concat_dim)
 
 
 def extended(cells, sides, width):
@@ -135,13 +158,7 @@
             concat_axis=0,
             tiled=True,
         ),
-        lax.all_to_all(
-            send_cells.reshape(peer_count, slot_count),
-            "space",
-            split_axis=0,
-            concat_axis=0,
-            tiled=True,
-        ),
+        sent_to_each(send_cells.reshape(peer_count, slot_count), "space", 0, 0),
     )
     recv_cells = recv_cells.reshape(-1)
     ocean_cells = ocn_one.shape[0]

time: 71.6 us -> 76.8 us (1.073)
  starting transfers between devices: 16.8 us -> 27.9 us
  blocking collectives: 31.6 us -> 22 us
  waiting for transfers between devices: 7.92 us -> 10.1 us
    ppermute x0 -> x7, starting transfers between devices: none -> 12.6 us  [sent_to_each(): lax.ppermute(sent, axis, [(i, (i + step) % count) for i in range(count)])]
    all_to_all x1 -> x0, blocking collectives: 10.6 us -> none  [local(): lax.all_to_all(send_rows.reshape(peer_count, slot_count, flux_width), 'sp...]
    all_to_all x1, starting transfers between devices: 6.96 us -> 3.41 us  [local(): lax.all_to_all(send_rows.reshape(peer_count, slot_count, flux_width), 'sp...]
    ppermute x0 -> x7, waiting for transfers between devices: none -> 2.09 us  [sent_to_each(): lax.ppermute(sent, axis, [(i, (i + step) % count) for i in range(count)])]
    all_to_all x1, starting transfers between devices: 3.54 us -> 5.56 us  [local(): lax.all_to_all(back_rows.reshape(peer_count, slot_count, flux_width), 'sp...]
    all_gather x1, blocking collectives: 21 us -> 22 us  [entering(): gathered = lax.all_gather(part, axis)]
  transfers between devices with their start and end apart: 4 -> 11, of which waited for: 1 -> 3; matrix products, arithmetic and copies ran while one was open for 13% -> 9% of each run, Pallas kernels for 0% -> 0%
where the time goes in v1:
time: 76.8 us; the launch traced here: 76.2 us
  starting transfers between devices  27.9 us (36%)
  blocking collectives  22 us (29%)
  waiting for transfers between devices  10.1 us (13%)
  matrix products  7.04 us (9%)
  local copies, waits for them, and re-layouts  5.27 us (7%)
  other arithmetic  2.61 us (3%)
  between operations  1.32 us (2%)
    all_gather x1, blocking collectives, entering(): gathered = lax.all_gather(part, axis)  22 us
    ppermute x7, starting transfers between devices, sent_to_each(): lax.ppermute(sent, axis, [(i, (i + step) % count) for i in range(count)])  12.6 us
    all_to_all x1, waiting for transfers between devices, local(): lax.all_to_all(back_rows.reshape(peer_count, slot_count, flux_width), 'sp...  7.98 us
    all_to_all x1, starting transfers between devices, local(): lax.all_to_all(back_rows.reshape(peer_count, slot_count, flux_width), 'sp...  5.56 us
    ppermute x1, starting transfers between devices, extended(): lax.ppermute(tail, axis, [(i, (i + 1) % count) for i in range(ends)])  5.01 us
    all_to_all x1, starting transfers between devices, local(): lax.all_to_all(send_rows.reshape(peer_count, slot_count, flux_width), 'sp...  3.41 us
    ppermute x7, waiting for transfers between devices, sent_to_each(): lax.ppermute(sent, axis, [(i, (i + step) % count) for i in range(count)])  2.09 us
    slice x6, local copies, waits for them, and re-layouts, conv_taps(): columns.append(jnp.roll(lat_band, 1 - col_off, axis=1))  1.81 us
  transfers between devices with their start and end apart: 11, of which 3 were waited for; matrix products, arithmetic and copies ran while one was open for 9% of the time, Pallas kernels for 0%

profile of v1, /device:TPU:0, one launch (start us, length us, event | category | flops | bytes accessed | tf_op | source)
XLA Modules:
  0.0 76.2 jit_solution(8975359639936924700)
XLA Ops:
  0.7 5.0 %collective-permute-start = (bf16[1,256,256]{2,1,0:T(8,128)(2,1)}, bf16[1,256,256]{2,1,0:T(8,128)(2,1)S(1)}, u32[]{:S(2)}, u32[]{:S(2)}) collective-permute-start(bf16[1,256,256]{2,1,0:T(8,128)(2,1)} %bitcast.109), channel_id=1, source_target_pairs={{0,2},{2,4},{4,6},{6,8},{8,10},{10,12},{12,14},{1,3},{3,5},{5,7},{... | collective-permute-start | bytes 393224 | tf_op jit(solution)/shard_map/ppermute | solution.py:39
  5.7 1.3 %collective-permute-start.1 = (bf16[1,256,256]{2,1,0:T(8,128)(2,1)}, bf16[1,256,256]{2,1,0:T(8,128)(2,1)S(1)}, u32[]{:S(2)}, u32[]{:S(2)}) collective-permute-start(bf16[1,256,256]{2,1,0:T(8,128)(2,1)} %bitcast.110), channel_id=1, source_target_pairs={{2,0},{4,2},{6,4},{8,6},{10,8},{12,10},{14,12},{3,1},{5,3},{7,5},{... | collective-permute-start | bytes 393224 | tf_op jit(solution)/shard_map/ppermute | solution.py:41
  7.0 1.0 %fusion.56 = (bf16[1,255,256]{2,1,0:T(8,128)(2,1)S(1)}, bf16[1,255,256]{2,1,0:T(8,128)(2,1)S(1)}) fusion(bf16[1,256,256]{2,1,0:T(8,128)(2,1)} %bitcast.111), kind=kLoop, calls=%fused_computation.96 | loop fusion | bytes 522240 | tf_op jit(solution)/shard_map/jit(_roll_static)/slice | solution.py:65
  8.0 0.7 fusion.57
  8.7 0.8 %copy.56 = s32[1,256,2]{2,1,0:T(8,128)S(1)} copy(s32[1,256,2]{1,2,0:T(2,128)} %param.22) | data formatting | bytes 4096 | tf_op args[2]
  9.9 0.7 convert_element_type.74
  10.6 1.1 %reduce-window.6 = s32[8,4,128]{2,0,1:T(8,128)S(1)} reduce-window(s32[8,4,128]{2,0,1:T(8,128)S(1)} %fusion.41, s32[]{:T(128)} %constant.90.clone.1), window={size=1x1x128 pad=0_0x0_0x127_0}, to_apply=%region_4.5 | reduce-window | flops 520192 | bytes 32772 | tf_op jit(solution)/shard_map/reduce-window
  13.9 22.0 %all-gather.1 = f32[8,1,256]{2,1,0:T(1,128)S(1)} all-gather(f32[1,1,256]{2,1,0:T(1,128)S(1)} %bitcast.127), channel_id=2, replica_groups=mesh['groups'=2,'space'=8,'section'=2] {'space'}, dimensions={0}, use_global_device_ids=true | all-gather | bytes 9216 | tf_op jit(solution)/shard_map/all_gather | solution.py:50
  37.4 1.6 %fusion.4 = bf16[1024,128]{1,0:T(8,128)(2,1)} fusion(s32[512]{0:T(512)S(1)} %multiply_add_fusion, f32[512,128]{1,0:T(8,128)S(1)} %bitcast.114, f32[512]{0:T(512)S(1)} %mul.149), kind=kOutput, calls=%fused_computation.8 | convolution fusion | flops 135004160 | bytes 528384 | tf_op jit(solution)/shard_map/dot_general | solution.py:83
  39.0 3.4 %all-to-all-start = ((bf16[8,128,128]{2,1,0:T(8,128)(2,1)}), bf16[8,128,128]{2,1,0:T(8,128)(2,1)S(1)}, u32[]{:S(2)}, u32[]{:S(2)}) async-start(bf16[8,128,128]{2,1,0:T(8,128)(2,1)} %bitcast.41), calls=%async_computation | async-start | bytes 524288 | tf_op jit(solution)/shard_map/all_to_all | solution.py:154
  42.8 2.0 %collective-permute-start.2 = (s32[1,128]{1,0:T(1,128)S(1)}, s32[1,128]{1,0:T(1,128)S(1)}, u32[]{:S(2)}, u32[]{:S(2)}) collective-permute-start(s32[1,128]{1,0:T(1,128)S(1)} %get-tuple-element.52), channel_id=1, source_target_pairs={{0,2},{2,4},{4,6},{6,8},{8,10},{10,12},{12,14},{14,0},{1,3},{3,5},... | collective-permute-start | bytes 1544 | tf_op jit(solution)/shard_map/ppermute | solution.py:26
  44.7 1.5 %collective-permute-start.3 = (s32[1,128]{1,0:T(1,128)S(1)}, s32[1,128]{1,0:T(1,128)S(1)}, u32[]{:S(2)}, u32[]{:S(2)}) collective-permute-start(s32[1,128]{1,0:T(1,128)S(1)} %get-tuple-element.51), channel_id=1, source_target_pairs={{0,4},{2,6},{4,8},{6,10},{8,12},{10,14},{12,0},{14,2},{1,5},{3,7},... | collective-permute-start | bytes 1544 | tf_op jit(solution)/shard_map/ppermute | solution.py:26
  46.2 2.4 %collective-permute-start.4 = (s32[1,128]{1,0:T(1,128)S(1)}, s32[1,128]{1,0:T(1,128)S(1)}, u32[]{:S(2)}, u32[]{:S(2)}) collective-permute-start(s32[1,128]{1,0:T(1,128)S(1)} %get-tuple-element.50), channel_id=1, source_target_pairs={{0,6},{2,8},{4,10},{6,12},{8,14},{10,0},{12,2},{14,4},{1,7},{3,9},... | collective-permute-start | bytes 1544 | tf_op jit(solution)/shard_map/ppermute | solution.py:26
  48.6 1.4 %collective-permute-start.5 = (s32[1,128]{1,0:T(1,128)S(1)}, s32[1,128]{1,0:T(1,128)S(1)}, u32[]{:S(2)}, u32[]{:S(2)}) collective-permute-start(s32[1,128]{1,0:T(1,128)S(1)} %get-tuple-element.49), channel_id=1, source_target_pairs={{0,8},{2,10},{4,12},{6,14},{8,0},{10,2},{12,4},{14,6},{1,9},{3,11}... | collective-permute-start | bytes 1544 | tf_op jit(solution)/shard_map/ppermute | solution.py:26
  50.0 2.4 %collective-permute-start.6 = (s32[1,128]{1,0:T(1,128)S(1)}, s32[1,128]{1,0:T(1,128)S(1)}, u32[]{:S(2)}, u32[]{:S(2)}) collective-permute-start(s32[1,128]{1,0:T(1,128)S(1)} %get-tuple-element.48), channel_id=1, source_target_pairs={{0,10},{2,12},{4,14},{6,0},{8,2},{10,4},{12,6},{14,8},{1,11},{3,13... | collective-permute-start | bytes 1544 | tf_op jit(solution)/shard_map/ppermute | solution.py:26
  52.5 1.5 %collective-permute-start.7 = (s32[1,128]{1,0:T(1,128)S(1)}, s32[1,128]{1,0:T(1,128)S(1)}, u32[]{:S(2)}, u32[]{:S(2)}) collective-permute-start(s32[1,128]{1,0:T(1,128)S(1)} %get-tuple-element.47), channel_id=1, source_target_pairs={{0,12},{2,14},{4,0},{6,2},{8,4},{10,6},{12,8},{14,10},{1,13},{3,15... | collective-permute-start | bytes 1544 | tf_op jit(solution)/shard_map/ppermute | solution.py:26
  54.0 1.5 %collective-permute-start.8 = (s32[1,128]{1,0:T(1,128)S(1)}, s32[1,128]{1,0:T(1,128)S(1)}, u32[]{:S(2)}, u32[]{:S(2)}) collective-permute-start(s32[1,128]{1,0:T(1,128)S(1)} %get-tuple-element.46), channel_id=1, source_target_pairs={{0,14},{2,0},{4,2},{6,4},{8,6},{10,8},{12,10},{14,12},{1,15},{3,1}... | collective-permute-start | bytes 1544 | tf_op jit(solution)/shard_map/ppermute | solution.py:26
  56.1 1.5 %collective-permute-done.8 = s32[1,128]{1,0:T(1,128)S(1)} collective-permute-done((s32[1,128]{1,0:T(1,128)S(1)}, s32[1,128]{1,0:T(1,128)S(1)}, u32[]{:S(2)}, u32[]{:S(2)}) %collective-permute-start.8) | collective-permute-done | bytes 544 | tf_op jit(solution)/shard_map/ppermute | solution.py:26
  58.1 0.8 %multiply_reduce_fusion.1 = (f32[256]{0:T(256)S(1)}, f32[256,192]{0,1:T(8,128)S(1)}) fusion(bf16[128,192]{0,1:T(8,128)(2,1)S(1)} %copy-done.12, bf16[1024,128]{1,0:T(8,128)(2,1)S(1)} %bitcast.115, s32[1024]{0:T(1024)S(1)} %bitcast.125, bf16[1,256,192]{1,2,0:T(8,128)(2,1)S(1)} %copy-done.11), kind=kOutput, calls=%fused_computation.38 | convolution fusion | flops 80183040 | bytes 611328 | tf_op jit(solution)/shard_map/dot_general | solution.py:169
  59.0 0.7 fusion.19
  59.8 1.2 %convolution_convert_fusion = bf16[1024,128]{1,0:T(8,128)(2,1)} fusion(bf16[256,192]{0,1:T(8,128)(2,1)S(1)} %fusion.19, bf16[192,128]{1,0:T(8,128)(2,1)S(1)} %copy-done.13, s32[1024]{0:T(1024)S(1)} %bitcast.126), kind=kOutput, calls=%fused_computation.9 | convolution fusion | flops 80117760 | bytes 413696 | tf_op jit(solution)/shard_map/dot_general | solution.py:182
  61.0 5.6 %all-to-all-start.1 = ((bf16[8,128,128]{2,1,0:T(8,128)(2,1)}), bf16[8,128,128]{2,1,0:T(8,128)(2,1)S(1)}, u32[]{:S(2)}, u32[]{:S(2)}) async-start(bf16[8,128,128]{2,1,0:T(8,128)(2,1)} %bitcast.43), calls=%async_computation.1 | async-start | bytes 524288 | tf_op jit(solution)/shard_map/all_to_all | solution.py:185
  66.8 8.0 %all-to-all-done.1 = bf16[8,128,128]{2,1,0:T(8,128)(2,1)S(1)} async-done(((bf16[8,128,128]{2,1,0:T(8,128)(2,1)}), bf16[8,128,128]{2,1,0:T(8,128)(2,1)S(1)}, u32[]{:S(2)}, u32[]{:S(2)}) %all-to-all-start.1) | async-done | bytes 262176 | tf_op jit(solution)/shard_map/all_to_all | solution.py:185
  75.3 0.8 %fusion.20 = bf16[1,1,256,256]{3,2,1,0:T(8,128)(2,1)} fusion(bf16[128,256]{1,0:T(8,128)(2,1)S(1)} %copy-done.4, bf16[256,256]{1,0:T(8,128)(2,1)S(1)} %fusion.18, f32[256]{0:T(256)S(1)} %bitcast.121, bf16[256,128]{1,0:T(8,128)(2,1)S(1)} %fusion.15), kind=kOutput, calls=%fused_computation.23 | convolution fusion | flops 17039360 | bytes 394240 | tf_op jit(solution)/shard_map/dot_general | solution.py:195
  (94 shorter events, 6.1 us)
Async XLA Ops:
  0.6 12.7 %copy-start = (bf16[9,256,256]{2,1,0:T(8,128)(2,1)S(1)}, bf16[9,256,256]{2,1,0:T(8,128)(2,1)}, u32[]{:S(2)}) copy-start(bf16[9,256,256]{2,1,0:T(8,128)(2,1)} %param.26) | copy-start | bytes 3538948
  0.7 11.9 %copy-start.5 = (s32[1,256,2]{1,2,0:T(2,128)S(1)}, s32[1,256,2]{1,2,0:T(2,128)}, u32[]{:S(2)}) copy-start(s32[1,256,2]{1,2,0:T(2,128)} %param.23) | copy-start | bytes 6148
  0.7 12.3 %collective-permute-start = (bf16[1,256,256]{2,1,0:T(8,128)(2,1)}, bf16[1,256,256]{2,1,0:T(8,128)(2,1)S(1)}, u32[]{:S(2)}, u32[]{:S(2)}) collective-permute-start(bf16[1,256,256]{2,1,0:T(8,128)(2,1)} %bitcast.109), channel_id=1, source_target_pairs={{0,2},{2,4},{4,6},{6,8},{8,10},{10,12},{12,14},{1,3},{3,5},{5,7},{... | collective-permute-start | bytes 393224 | tf_op jit(solution)/shard_map/ppermute | solution.py:39
  5.7 7.5 %collective-permute-start.1 = (bf16[1,256,256]{2,1,0:T(8,128)(2,1)}, bf16[1,256,256]{2,1,0:T(8,128)(2,1)S(1)}, u32[]{:S(2)}, u32[]{:S(2)}) collective-permute-start(bf16[1,256,256]{2,1,0:T(8,128)(2,1)} %bitcast.110), channel_id=1, source_target_pairs={{2,0},{4,2},{6,4},{8,6},{10,8},{12,10},{14,12},{3,1},{5,3},{7,5},{... | collective-permute-start | bytes 393224 | tf_op jit(solution)/shard_map/ppermute | solution.py:41
  13.4 22.5 %copy-start.2 = (bf16[256,256]{1,0:T(8,128)(2,1)S(1)}, bf16[256,256]{1,0:T(8,128)(2,1)}, u32[]{:S(2)}) copy-start(bf16[256,256]{1,0:T(8,128)(2,1)} %param.27) | copy-start | bytes 393220
  13.4 22.9 %copy-start.7 = (bf16[1024,256]{1,0:T(8,128)(2,1)S(1)}, bf16[1024,256]{1,0:T(8,128)(2,1)}, u32[]{:S(2)}) copy-start(bf16[1024,256]{1,0:T(8,128)(2,1)} %param.30) | copy-start | bytes 1572868
  13.4 22.9 %copy-start.8 = (bf16[256,1024]{1,0:T(8,128)(2,1)S(1)}, bf16[256,1024]{1,0:T(8,128)(2,1)}, u32[]{:S(2)}) copy-start(bf16[256,1024]{1,0:T(8,128)(2,1)} %param.29) | copy-start | bytes 1572868
  13.4 22.9 %copy-start.14 = (f32[256]{0:T(256)S(1)}, f32[256]{0:T(256)}, u32[]{:S(2)}) copy-start(f32[256]{0:T(256)} %param.28) | copy-start | bytes 3076
  37.1 21.0 %copy-start.11 = (bf16[1,256,192]{1,2,0:T(8,128)(2,1)S(1)}, bf16[1,256,192]{1,2,0:T(8,128)(2,1)}, u32[]{:S(2)}) copy-start(bf16[1,256,192]{1,2,0:T(8,128)(2,1)} %param.21) | copy-start | bytes 294916
  37.1 21.0 %copy-start.12 = (bf16[128,192]{0,1:T(8,128)(2,1)S(1)}, bf16[128,192]{0,1:T(8,128)(2,1)}, u32[]{:S(2)}) copy-start(bf16[128,192]{0,1:T(8,128)(2,1)} %param.32) | copy-start | bytes 147460
  37.4 21.6 %copy-start.9 = (bf16[768,192]{0,1:T(8,128)(2,1)S(1)}, bf16[768,192]{0,1:T(8,128)(2,1)}, u32[]{:S(2)}) copy-start(bf16[768,192]{0,1:T(8,128)(2,1)} %param.35) | copy-start | bytes 884740
  37.4 21.5 %copy-start.10 = (bf16[192,768]{1,0:T(8,128)(2,1)S(1)}, bf16[192,768]{1,0:T(8,128)(2,1)}, u32[]{:S(2)}) copy-start(bf16[192,768]{1,0:T(8,128)(2,1)} %param.34) | copy-start | bytes 884740
  37.4 21.5 %copy-start.15 = (f32[192]{0:T(256)S(1)}, f32[192]{0:T(256)}, u32[]{:S(2)}) copy-start(f32[192]{0:T(256)} %param.33) | copy-start | bytes 2308
  39.0 19.1 %all-to-all-start = ((bf16[8,128,128]{2,1,0:T(8,128)(2,1)}), bf16[8,128,128]{2,1,0:T(8,128)(2,1)S(1)}, u32[]{:S(2)}, u32[]{:S(2)}) async-start(bf16[8,128,128]{2,1,0:T(8,128)(2,1)} %bitcast.41), calls=%async_computation | async-start | bytes 524288 | tf_op jit(solution)/shard_map/all_to_all | solution.py:154
  42.8 9.7 %collective-permute-start.2 = (s32[1,128]{1,0:T(1,128)S(1)}, s32[1,128]{1,0:T(1,128)S(1)}, u32[]{:S(2)}, u32[]{:S(2)}) collective-permute-start(s32[1,128]{1,0:T(1,128)S(1)} %get-tuple-element.52), channel_id=1, source_target_pairs={{0,2},{2,4},{4,6},{6,8},{8,10},{10,12},{12,14},{14,0},{1,3},{3,5},... | collective-permute-start | bytes 1544 | tf_op jit(solution)/shard_map/ppermute | solution.py:26
  44.7 9.2 %collective-permute-start.3 = (s32[1,128]{1,0:T(1,128)S(1)}, s32[1,128]{1,0:T(1,128)S(1)}, u32[]{:S(2)}, u32[]{:S(2)}) collective-permute-start(s32[1,128]{1,0:T(1,128)S(1)} %get-tuple-element.51), channel_id=1, source_target_pairs={{0,4},{2,6},{4,8},{6,10},{8,12},{10,14},{12,0},{14,2},{1,5},{3,7},... | collective-permute-start | bytes 1544 | tf_op jit(solution)/shard_map/ppermute | solution.py:26
  46.2 9.2 %collective-permute-start.4 = (s32[1,128]{1,0:T(1,128)S(1)}, s32[1,128]{1,0:T(1,128)S(1)}, u32[]{:S(2)}, u32[]{:S(2)}) collective-permute-start(s32[1,128]{1,0:T(1,128)S(1)} %get-tuple-element.50), channel_id=1, source_target_pairs={{0,6},{2,8},{4,10},{6,12},{8,14},{10,0},{12,2},{14,4},{1,7},{3,9},... | collective-permute-start | bytes 1544 | tf_op jit(solution)/shard_map/ppermute | solution.py:26
  48.6 6.8 %collective-permute-start.5 = (s32[1,128]{1,0:T(1,128)S(1)}, s32[1,128]{1,0:T(1,128)S(1)}, u32[]{:S(2)}, u32[]{:S(2)}) collective-permute-start(s32[1,128]{1,0:T(1,128)S(1)} %get-tuple-element.49), channel_id=1, source_target_pairs={{0,8},{2,10},{4,12},{6,14},{8,0},{10,2},{12,4},{14,6},{1,9},{3,11}... | collective-permute-start | bytes 1544 | tf_op jit(solution)/shard_map/ppermute | solution.py:26
  50.0 5.4 %collective-permute-start.6 = (s32[1,128]{1,0:T(1,128)S(1)}, s32[1,128]{1,0:T(1,128)S(1)}, u32[]{:S(2)}, u32[]{:S(2)}) collective-permute-start(s32[1,128]{1,0:T(1,128)S(1)} %get-tuple-element.48), channel_id=1, source_target_pairs={{0,10},{2,12},{4,14},{6,0},{8,2},{10,4},{12,6},{14,8},{1,11},{3,13... | collective-permute-start | bytes 1544 | tf_op jit(solution)/shard_map/ppermute | solution.py:26
  52.5 3.6 %collective-permute-start.7 = (s32[1,128]{1,0:T(1,128)S(1)}, s32[1,128]{1,0:T(1,128)S(1)}, u32[]{:S(2)}, u32[]{:S(2)}) collective-permute-start(s32[1,128]{1,0:T(1,128)S(1)} %get-tuple-element.47), channel_id=1, source_target_pairs={{0,12},{2,14},{4,0},{6,2},{8,4},{10,6},{12,8},{14,10},{1,13},{3,15... | collective-permute-start | bytes 1544 | tf_op jit(solution)/shard_map/ppermute | solution.py:26
  54.0 3.6 %collective-permute-start.8 = (s32[1,128]{1,0:T(1,128)S(1)}, s32[1,128]{1,0:T(1,128)S(1)}, u32[]{:S(2)}, u32[]{:S(2)}) collective-permute-start(s32[1,128]{1,0:T(1,128)S(1)} %get-tuple-element.46), channel_id=1, source_target_pairs={{0,14},{2,0},{4,2},{6,4},{8,6},{10,8},{12,10},{14,12},{1,15},{3,1}... | collective-permute-start | bytes 1544 | tf_op jit(solution)/shard_map/ppermute | solution.py:26
  59.8 15.6 %copy-start.16 = (bf16[256,192]{0,1:T(8,128)(2,1)}, bf16[256,192]{0,1:T(8,128)(2,1)S(1)}, u32[]{:S(2)}) copy-start(bf16[256,192]{0,1:T(8,128)(2,1)S(1)} %fusion.19) | copy-start | bytes 294916
  61.0 14.3 %copy-start.4 = (bf16[128,256]{1,0:T(8,128)(2,1)S(1)}, bf16[128,256]{1,0:T(8,128)(2,1)}, u32[]{:S(2)}) copy-start(bf16[128,256]{1,0:T(8,128)(2,1)} %param.37) | copy-start | bytes 196612
  61.0 13.8 %all-to-all-start.1 = ((bf16[8,128,128]{2,1,0:T(8,128)(2,1)}), bf16[8,128,128]{2,1,0:T(8,128)(2,1)S(1)}, u32[]{:S(2)}, u32[]{:S(2)}) async-start(bf16[8,128,128]{2,1,0:T(8,128)(2,1)} %bitcast.43), calls=%async_computation.1 | async-start | bytes 524288 | tf_op jit(solution)/shard_map/all_to_all | solution.py:185
  (4 other events, 14.0 us)
